TPU v7x, 32 devices: a whole 2x2x4 slice. The times are simulated.
32 devices in a mesh: row: 8 (over z, core), col: 4 (over y, x).
Axes of the slice: x: 2, y: 2, z: 4, core: 2. Of those that a mesh axis runs over, the one named last changes fastest.
Arguments:
- features: bfloat16 [9, 1, 128, 128, 128], P(None, None, 'row', 'col'), may hold values from -12 to 12
- cotangent: float32 [3, 1, 128, 128, 128], P(None, None, 'row', 'col'), may hold values from -14 to 14
- w_in: bfloat16 [9, 256], replicated, may hold values from -2 to 2
- bias_in: float32 [256], replicated, may hold values from -3 to 3
- w_mid: bfloat16 [256, 256], replicated, may hold values from -0.375 to 0.375
- bias_mid: float32 [256], replicated, may hold values from -3 to 3
- w_out: bfloat16 [256, 6], replicated, may hold values from -2.5 to 2.5
Outputs:
- grad_features: float32 [9, 1, 128, 128, 128], P(None, None, 'row', 'col')
- grad_w_in: float32 [9, 256], replicated
- grad_b_in: float32 [256], replicated
- grad_w_mid: float32 [256, 256], replicated
- grad_b_mid: float32 [256], replicated
- grad_w_out: float32 [256, 6], replicated
All inputs are finite; a program needn't handle non-finite values.
Results may differ from a plain program's by a relative error of at most 0.025.
Values sent between devices are 32-bit elements; how exact they have to be, the bound alone decides.
A program may use at most 128 MiB of HBM per device.

v0:
```python
import math
import jax
import jax.numpy as jnp
from jax import lax
from jax.sharding import PartitionSpec as P

NX = 128
NY = 128
NZ = 128
CELLS = 2097152
STEP_DT = 0.04
PAIRS = ((0, 0), (1, 1), (2, 2), (0, 1), (0, 2), (1, 2))


def mode_list(count, length):
    index = jnp.arange(count, dtype=jnp.int32)
    return jnp.where(index < length // 2, index, index - length)


def phase_table(modes, length):
    positions = jnp.arange(length, dtype=jnp.int32)
    turns = positions[:, None] * modes[None, :] % length
    angle = turns.astype(jnp.float32) * (2.0 * math.pi / length)
    return (jnp.cos(angle), jnp.sin(angle))


def contract(form, left, right):
    return jnp.einsum(
        form, left, right, precision=lax.Precision.HIGHEST, preferred_element_type=jnp.float32
    )


def complex_product(form, part, table_real, table_imag):
    real = contract(form, part[0], table_real) - contract(form, part[1], table_imag)
    imag = contract(form, part[0], table_imag) + contract(form, part[1], table_real)
    return jnp.stack([real, imag])


def closure_block(x_blk, g_blk, w_in, bias_in, w_mid, bias_mid, w_out):
    pre_in = (
        jnp.einsum("fh,fn->hn", w_in, x_blk, preferred_element_type=jnp.float32) + bias_in[:, None]
    )
    act_in = jnp.tanh(pre_in).astype(jnp.bfloat16)
    pre_mid = (
        jnp.einsum("io,in->on", w_mid, act_in, preferred_element_type=jnp.float32)
        + bias_mid[:, None]
    )
    act_mid = jnp.tanh(pre_mid).astype(jnp.bfloat16)
    back_mid = jnp.einsum("ho,on->hn", w_out, g_blk, preferred_element_type=jnp.float32)
    delta_mid = (back_mid * (1.0 - jnp.square(act_mid.astype(jnp.float32)))).astype(jnp.bfloat16)
    back_in = jnp.einsum("io,on->in", w_mid, delta_mid, preferred_element_type=jnp.float32)
    delta_in = (back_in * (1.0 - jnp.square(act_in.astype(jnp.float32)))).astype(jnp.bfloat16)
    grad_x = jnp.einsum("fh,hn->fn", w_in, delta_in, preferred_element_type=jnp.float32)
    gw_out = jnp.einsum("hn,on->ho", act_mid, g_blk, preferred_element_type=jnp.float32)
    gw_mid = jnp.einsum("in,on->io", act_in, delta_mid, preferred_element_type=jnp.float32)
    gw_in = jnp.einsum("fn,hn->fh", x_blk, delta_in, preferred_element_type=jnp.float32)
    gb_mid = jnp.sum(delta_mid.astype(jnp.float32), axis=1)
    gb_in = jnp.sum(delta_in.astype(jnp.float32), axis=1)
    return (grad_x, (gw_in, gb_in, gw_mid, gb_mid, gw_out))


def per_device(features, cotangent, w_in, bias_in, w_mid, bias_mid, w_out):
    rows_group = lax.axis_size("row")
    cols_group = lax.axis_size("col")
    count_y = NY
    count_z = NZ
    list_z = mode_list(count_z, NZ)
    weight_z = jnp.ones((count_z,), jnp.float32) / NZ
    list_x = mode_list(NX, NX)
    list_y = mode_list(count_y, NY)
    cos_x, sin_x = phase_table(list_x, NX)
    cos_y, sin_y = phase_table(list_y, NY)
    cos_z, sin_z = phase_table(list_z, NZ)
    forward_z = jnp.stack(
        [
            contract("csxyz,zk->csxky", cotangent, cos_z),
            -contract("csxyz,zk->csxky", cotangent, sin_z),
        ]
    )
    spectra = complex_product(
        "csxky,yq->cskqx",
        lax.all_to_all(forward_z, "col", split_axis=4, concat_axis=5, tiled=True),
        cos_y,
        -sin_y,
    )
    spectra = complex_product(
        "cskqx,xp->cskqp",
        lax.all_to_all(spectra, "row", split_axis=4, concat_axis=5, tiled=True),
        cos_x,
        -sin_x,
    )
    share_y = count_y // rows_group
    share_z = count_z // cols_group
    local_y = lax.dynamic_slice_in_dim(list_y, lax.axis_index("row") * share_y, share_y)
    local_z = lax.dynamic_slice_in_dim(list_z, lax.axis_index("col") * share_z, share_z)
    modes_x = list_x[None, None, :]
    modes_y = local_y[None, :, None]
    modes_z = local_z[:, None, None]
    keep = (3 * jnp.abs(modes_x) < NX) & (3 * jnp.abs(modes_y) < NY) & (3 * jnp.abs(modes_z) < NZ)
    waves = [modes_x.astype(jnp.float32), modes_y.astype(jnp.float32), modes_z.astype(jnp.float32)]
    velocity = [spectra[:, comp] for comp in range(3)]
    inner = waves[0] * velocity[0] + waves[1] * velocity[1] + waves[2] * velocity[2]
    square = jnp.maximum(waves[0] * waves[0] + waves[1] * waves[1] + waves[2] * waves[2], 1.0)
    projected = [
        jnp.where(keep, velocity[comp] - waves[comp] * inner / square, 0.0) for comp in range(3)
    ]
    stress_parts = []
    for first, second in PAIRS:
        if first == second:
            value = waves[first] * projected[first]
        else:
            value = waves[second] * projected[first] + waves[first] * projected[second]
        stress_parts.append(jnp.stack([-STEP_DT * value[1], STEP_DT * value[0]]))
    stress_hat = jnp.stack(stress_parts, axis=1)
    back_x = complex_product("cskqp,px->cskxq", stress_hat, cos_x.T / NX, sin_x.T / NX)
    stress_mid = complex_product(
        "cskxq,qy->csxyk",
        lax.all_to_all(back_x, "row", split_axis=4, concat_axis=5, tiled=True),
        cos_y.T / NY,
        sin_y.T / NY,
    )
    real_z = cos_z.T * weight_z[:, None]
    imag_z = sin_z.T * weight_z[:, None]
    part = lax.all_to_all(stress_mid, "col", split_axis=4, concat_axis=5, tiled=True)
    stress = contract("csxyk,kz->csxyz", part[0], real_z) - contract(
        "csxyk,kz->csxyz", part[1], imag_z
    )
    inputs_count = features.shape[0]
    stress_count = stress.shape[0]
    cells = stress.shape[1] * stress.shape[2] * stress.shape[3] * stress.shape[4]
    feats = features.reshape(inputs_count, cells)
    grads = stress.astype(jnp.bfloat16).reshape(stress_count, cells)
    hidden = w_mid.shape[0]
    blank = jnp.zeros((inputs_count, cells), jnp.float32)
    block = math.gcd(cells, max(1024, cells // 8))

    def visit(index, carry):
        current, totals = carry
        start = (0 + index * block).astype(jnp.int32)
        x_blk = lax.dynamic_slice_in_dim(feats, start, block, 1)
        g_blk = lax.dynamic_slice_in_dim(grads, start, block, 1)
        grad_x, parts = closure_block(x_blk, g_blk, w_in, bias_in, w_mid, bias_mid, w_out)
        current = lax.dynamic_update_slice_in_dim(current, grad_x, start, 1)
        return (current, tuple((a + b for a, b in zip(totals, parts))))

    init = (
        jnp.zeros((inputs_count, hidden), jnp.float32),
        jnp.zeros((hidden,), jnp.float32),
        jnp.zeros((hidden, hidden), jnp.float32),
        jnp.zeros((hidden,), jnp.float32),
        jnp.zeros((hidden, stress_count), jnp.float32),
    )
    field, local = lax.fori_loop(0, cells // block, visit, (blank, init))
    totals = lax.psum((local[0], local[1], local[2], local[3], local[4]), ("row", "col"))
    factor = 1.0 / math.sqrt(CELLS)
    return (
        field.reshape(features.shape),
        totals[0] * factor,
        totals[1] * factor,
        totals[2] * factor,
        totals[3] * factor,
        totals[4] * factor,
    )


def solution(mesh):
    return jax.shard_map(
        per_device,
        mesh=mesh,
        in_specs=(
            P(None, None, "row", "col", None),
            P(None, None, "row", "col", None),
            P(),
            P(),
            P(),
            P(),
            P(),
        ),
        out_specs=(P(None, None, "row", "col", None), P(), P(), P(), P(), P()),
        check_vma=False,
    )
```

profile of v0, /device:TPU:0, one launch (start us, length us, event | category | flops | bytes accessed | tf_op | source)
XLA Modules:
  0.0 856.4 jit_solution(18035341283685795229)
XLA Ops:
  10.6 6.0 copy.51
  22.5 25.4 %all_to_all.60 = f32[4,1,98304]{2,1,0:T(1,128)S(1)} all-to-all(f32[4,1,98304]{2,1,0:T(1,128)} %reshape.562), channel_id=1, replica_groups=mesh['row'=8,'col'=4] {'col'}, dimensions={0} | all-to-all | bytes 3145728 | tf_op jit(solution)/shard_map/all_to_all | solution.py:82
  48.4 6.4 reduce.2
  54.7 6.3 reshape.563
  61.0 6.8 copy.95
  81.1 6.0 copy.53
  87.1 7.6 reshape.564
  100.6 36.9 %all-to-all-done.1 = f32[8,1,49152]{2,1,0:T(1,128)S(1)} async-done(((f32[8,1,49152]{2,1,0:T(1,128)}), f32[8,1,49152]{2,1,0:T(1,128)S(1)}, u32[]{:S(2)}, u32[]{:S(2)}) %all-to-all-start.1) | async-done | bytes 1572896 | tf_op jit(solution)/shard_map/all_to_all | solution.py:88
  137.5 6.2 reduce.3
  143.7 6.1 reshape.565
  186.4 11.4 %copy.63 = f32[2,6,1,32,128,16]{3,5,1,2,0,4:T(8,128)} copy(f32[2,6,1,32,128,16]{4,3,5,1,2,0:T(8,128)} %pad_maximum_fusion) | data formatting | bytes 6291456 | tf_op jit(solution)/shard_map/stack | solution.py:36
  197.8 10.6 %reshape.566 = f32[8,1,98304]{2,1,0:T(1,128)} reshape(f32[128,2,1,6,16,32]{5,4,3,2,1,0:T(8,128)} %bitcast.283) | data formatting | bytes 6291456
  208.5 76.0 %all_to_all.61 = f32[8,1,98304]{2,1,0:T(1,128)} all-to-all(f32[8,1,98304]{2,1,0:T(1,128)} %reshape.566), channel_id=1, replica_groups=mesh['row'=8,'col'=4] {'row'}, dimensions={0} | all-to-all | bytes 6291456 | tf_op jit(solution)/shard_map/all_to_all | solution.py:118
  284.4 11.7 %reduce.4 = f32[8,98304]{1,0:T(8,128)} reduce(f32[8,1,98304]{2,1,0:T(1,128)} %all_to_all.61, f32[]{:T(128)} %broadcast.808), dimensions={1}, to_apply=%all_to_all.50.reduce_sub_computation | reduce | bytes 6291460 | tf_op jit(solution)/shard_map/all_to_all | solution.py:118
  296.1 10.9 %reshape.567 = f32[128,2,1,6,16,32]{5,4,3,2,1,0:T(8,128)} reshape(f32[8,98304]{1,0:T(8,128)} %reduce.4) | data formatting | bytes 6291456
  307.0 10.4 %copy.64 = f32[2,6,1,32,128,16]{3,5,4,1,0,2:T(8,128)} copy(f32[2,6,1,32,128,16]{3,5,1,2,0,4:T(8,128)} %bitcast.281) | data formatting | bytes 6291456 | tf_op jit(solution)/shard_map/all_to_all | solution.py:118
  317.4 10.7 %fusion.205 = (f32[1,6,1,32,16,8,16]{3,6,4,5,1,0,2:T(8,128)}, f32[1,6,1,32,16,8,16]{3,6,4,5,1,0,2:T(8,128)}) fusion(f32[2,6,1,32,16,8,16]{3,6,4,5,1,0,2:T(8,128)} %bitcast.279), kind=kLoop, calls=%fused_computation.273 | loop fusion | bytes 6291456 | tf_op jit(solution)/shard_map/slice | solution.py:34
  331.8 10.1 %fusion.64 = f32[128,6,32,16]{0,2,3,1:T(8,128)S(1)} fusion(f32[6,32,16,128]{1,3,2,0:T(8,128)S(1)} %bitcast.277, s32[128]{0:T(128)S(1)} %compare_select_fusion), kind=kOutput, calls=%fused_computation.138 | convolution fusion | flops 604225536 | bytes 3146240 | tf_op jit(solution)/shard_map/cskxq,qy->csxyk/dot_general | solution.py:28
  341.9 10.2 %fusion.43 = f32[128,6,32,16]{0,2,3,1:T(8,128)S(1)} fusion(f32[6,32,16,128]{1,3,2,0:T(8,128)S(1)} %bitcast.278, s32[128]{0:T(128)S(1)} %compare_select_fusion), kind=kOutput, calls=%fused_computation.117 | convolution fusion | flops 604225536 | bytes 3146240 | tf_op jit(solution)/shard_map/cskxq,qy->csxyk/dot_general | solution.py:28
  353.1 10.5 %subtract_bitcast_fusion = f32[1,6,1,16,128,32]{4,5,3,1,2,0:T(8,128)S(1)} fusion(f32[128,6,32,16]{0,2,3,1:T(8,128)S(1)} %fusion.64, f32[6,32,16,128]{1,3,2,0:T(8,128)S(1)} %bitcast.275, s32[128]{0:T(128)S(1)} %compare_select_fusion), kind=kOutput, calls=%fused_computation.41 | convolution fusion | flops 604618752 | bytes 4719104 | tf_op jit(solution)/shard_map/cskxq,qy->csxyk/dot_general | solution.py:28
  363.6 10.1 %add_bitcast_fusion = f32[1,6,1,16,128,32]{4,5,3,1,2,0:T(8,128)S(1)} fusion(f32[128,6,32,16]{0,2,3,1:T(8,128)S(1)} %fusion.43, f32[6,32,16,128]{1,3,2,0:T(8,128)S(1)} %bitcast.276, s32[128]{0:T(128)S(1)} %compare_select_fusion), kind=kOutput, calls=%fused_computation.40 | convolution fusion | flops 604618752 | bytes 4719104 | tf_op jit(solution)/shard_map/cskxq,qy->csxyk/dot_general | solution.py:28
  375.7 11.4 %copy.71 = f32[2,6,1,16,128,32]{5,3,1,2,0,4:T(8,128)} copy(f32[2,6,1,16,128,32]{4,5,3,1,2,0:T(8,128)} %pad_maximum_fusion.1) | data formatting | bytes 6291456 | tf_op jit(solution)/shard_map/stack | solution.py:36
  387.1 9.3 %reshape.568 = f32[4,1,196608]{2,1,0:T(1,128)} reshape(f32[128,2,1,6,16,32]{5,4,3,2,1,0:T(8,128)} %bitcast.284) | data formatting | bytes 6291456
  404.2 33.1 %all-to-all-done.3 = f32[4,1,196608]{2,1,0:T(1,128)} async-done(((f32[4,1,196608]{2,1,0:T(1,128)}), f32[4,1,196608]{2,1,0:T(1,128)}, u32[]{:S(2)}, u32[]{:S(2)}) %all-to-all-start.3) | async-done | bytes 3145760 | tf_op jit(solution)/shard_map/all_to_all | solution.py:124
  437.3 11.8 %reduce.5 = f32[4,196608]{1,0:T(4,128)} reduce(f32[4,1,196608]{2,1,0:T(1,128)} %all-to-all-done.3, f32[]{:T(128)} %broadcast.808), dimensions={1}, to_apply=%all_to_all.53.reduce_sub_computation | reduce | bytes 6291460 | tf_op jit(solution)/shard_map/all_to_all | solution.py:124
  449.1 10.7 %reshape.569 = f32[128,2,1,6,16,32]{5,4,3,2,1,0:T(8,128)} reshape(f32[4,196608]{1,0:T(4,128)} %reduce.5) | data formatting | bytes 6291456
  459.9 16.4 %copy.94 = f32[2,6,1,16,4,32,32]{6,4,5,3,1,2,0:T(4,128)} copy(f32[2,6,1,16,4,32,32]{6,3,1,0,5,4,2:T(8,128)} %bitcast.282) | data formatting | bytes 6291456 | tf_op jit(solution)/shard_map/all_to_all | solution.py:124
  476.3 14.3 %fusion.204 = (f32[1,6,1,16,32,4,32]{6,5,4,3,1,2,0:T(4,128)}, f32[1,6,1,16,32,4,32]{6,5,4,3,1,2,0:T(4,128)}) fusion(f32[2,6,1,16,32,4,32]{6,5,4,3,1,2,0:T(4,128)} %bitcast.280), kind=kLoop, calls=%fused_computation.272 | loop fusion | bytes 6291456 | tf_op jit(solution)/shard_map/slice | solution.py:126
  490.7 6.0 reshape.552
  511.5 165.8 %while.24 = (s32[]{:T(128)}, f32[9,65536]{1,0:T(8,128)}, f32[9,256]{1,0:T(8,128)S(1)}, f32[256]{0:T(256)S(1)}, f32[256,256]{1,0:T(8,128)S(1)}, /*index=5*/f32[25...) while((s32[]{:T(128)}, f32[9,65536]{1,0:T(8,128)}, ...), condition=%wide.region_3.4_spmd.clone, body=%wide.region_0.3_spmd.clone.sunk | while | flops 3422691328 | bytes 157343136 | solution.py:153
  677.3 37.5 %all-reduce = (f32[9,256]{1,0:T(8,128)S(1)}, f32[256]{0:T(256)S(1)}, f32[256]{0:T(256)S(1)}, f32[256,6]{0,1:T(8,128)S(1)}) all-reduce(f32[9,256]{1,0:T(8,128)S(1)} %get-tuple-element.241, f32[256]{0:T(256)S(1)} %get-tuple-element.242, f32[256]{0:T(256)S(1)} %get-tuple-element.244, ...), channel_id=1, replica_groups=mesh['row'=8,'col'=4] {'row','col'}, use_global_device_ids=true, to_apply=%region_4.5 | all-reduce | flops 4352 | bytes 34816 | tf_op jit(solution)/shard_map/psum | solution.py:154
  721.8 125.8 %all-reduce.3.cloned.1.call-done = f32[256,256]{1,0:T(8,128)} async-done(((f32[256,256]{1,0:T(8,128)}), f32[256,256]{1,0:T(8,128)}) %all-reduce.3.cloned.1.call-update) | async-done | bytes 262160 | tf_op jit(solution)/shard_map/psum | solution.py:154
  (268 shorter events, 267.9 us)
Async XLA Ops:
  94.7 42.8 %all-to-all-start.1 = ((f32[8,1,49152]{2,1,0:T(1,128)}), f32[8,1,49152]{2,1,0:T(1,128)S(1)}, u32[]{:S(2)}, u32[]{:S(2)}) async-start(f32[8,1,49152]{2,1,0:T(1,128)} %reshape.564), calls=%async_computation.1 | async-start | bytes 3145728 | tf_op jit(solution)/shard_map/all_to_all | solution.py:88
  331.8 20.3 %slice-start = ((s8[6291456]{0:T(1024)(128)(4,1)}), s8[4194304]{0:T(1024)(128)(4,1)S(1)}, s32[]{:S(2)}) async-start(s8[6291456]{0:T(1024)(128)(4,1)} %bitcast.291), calls=%async_computation.5 | async-start | bytes 8388608
  341.9 10.3 %slice-start.1 = ((s8[6291456]{0:T(1024)(128)(4,1)}), s8[2097152]{0:T(1024)(128)(4,1)S(1)}, s32[]{:S(2)}) async-start(s8[6291456]{0:T(1024)(128)(4,1)} %bitcast.291), calls=%async_computation.6 | async-start | bytes 4194304
  396.4 4.9 copy-start.9
  396.4 40.9 %all-to-all-start.3 = ((f32[4,1,196608]{2,1,0:T(1,128)}), f32[4,1,196608]{2,1,0:T(1,128)}, u32[]{:S(2)}, u32[]{:S(2)}) async-start(f32[4,1,196608]{2,1,0:T(1,128)} %reshape.568), calls=%async_computation.3 | async-start | bytes 6291456 | tf_op jit(solution)/shard_map/all_to_all | solution.py:124
  401.2 446.4 %all-reduce.3.cloned.1.call-start = ((), (), s32[]{:S(2)}) async-start(), calls=%async_computation.4 | async-start | bytes 524288 | tf_op jit(solution)/shard_map/psum | solution.py:154
  517.5 4.0 copy-start.5
  521.4 4.4 copy-start.4
  525.8 3.7 copy-start.2
  538.2 4.0 copy-start.5
  542.1 4.4 copy-start.4
  546.5 3.7 copy-start.2
  558.8 4.0 copy-start.5
  562.8 4.4 copy-start.4
  567.2 3.7 copy-start.2
  579.5 4.0 copy-start.5
  583.5 4.4 copy-start.4
  587.9 3.7 copy-start.2
  600.2 4.0 copy-start.5
  604.2 4.4 copy-start.4
  608.6 3.7 copy-start.2
  620.9 4.0 copy-start.5
  624.9 4.4 copy-start.4
  629.3 3.7 copy-start.2
  641.6 4.0 copy-start.5
  645.6 4.4 copy-start.4
  650.0 3.7 copy-start.2
  662.3 4.0 copy-start.5
  666.3 4.3 copy-start.4
  670.6 3.7 copy-start.2
  677.3 42.4 %copy-start.8 = (f32[256,256]{1,0:T(8,128)}, f32[256,256]{1,0:T(8,128)S(1)}, u32[]{:S(2)}) copy-start(f32[256,256]{1,0:T(8,128)S(1)} %get-tuple-element.243) | copy-start | bytes 786436
  716.5 132.8 %copy-start.1 = (f32[3,1,16,32,128]{4,3,2,1,0:T(8,128)S(1)}, f32[3,1,16,32,128]{4,3,2,1,0:T(8,128)}, u32[]{:S(2)}) copy-start(f32[3,1,16,32,128]{4,3,2,1,0:T(8,128)} %param.10) | copy-start | bytes 2359300
  (30 other events, 76.6 us)
Sparse Core Ops, SparseCore 0:
  721.3 126.2 all-reduce.2
where the time goes:
time: 862 us; the launch traced here: 856 us
  matrix products  242 us (28%)
  local copies, waits for them, and re-layouts  207 us (24%)
  waiting for transfers between devices  196 us (23%)
  blocking collectives  139 us (16%)
  other arithmetic  46.9 us (5%)
  between operations  14.9 us (2%)
  starting transfers between devices  9.97 us (1%)
    psum x1, waiting for transfers between devices, per_device(): lax.psum((local[0], local[1], local[2], local[3], local[4]), ('row', 'col'))  126 us
    dot_general x20, matrix products, contract(): jnp.einsum(form, left, right, precision=lax.Precision.HIGHEST, preferred_...  81.1 us
    unnamed x35, local copies, waits for them, and re-layouts  76.7 us
    all_to_all x1, blocking collectives, per_device(): lax.all_to_all(back_x, 'row', split_axis=4, concat_axis=5, tiled=True)  76 us
    psum x1, blocking collectives, per_device(): lax.psum((local[0], local[1], local[2], local[3], local[4]), ('row', 'col'))  37.5 us
    all_to_all x1, waiting for transfers between devices, per_device(): lax.all_to_all(spectra, 'row', split_axis=4, concat_axis=5, tiled=True)  36.9 us
    dot_general x8, matrix products, closure_block(): jnp.einsum('fh,hn->fn', w_in, delta_in, preferred_element_type=jnp.float32)  34.8 us
    all_to_all x1, waiting for transfers between devices, per_device(): lax.all_to_all(stress_mid, 'col', split_axis=4, concat_axis=5, tiled=True)  33.1 us
  transfers between devices with their start and end apart: 3, of which 3 were waited for; matrix products, arithmetic and copies ran while one was open for 0% of the time, Pallas kernels for 0%

commit v1 on v0

--- a/solution.py
+++ b/solution.py
@@ -151,7 +151,8 @@
         jnp.zeros((hidden, stress_count), jnp.float32),
     )
     field, local = lax.fori_loop(0, cells // block, visit, (blank, init))
-    totals = lax.psum((local[0], local[1], local[2], local[3], local[4]), ("row", "col"))
+    half = lax.psum((local[0], local[1], local[2], local[3], local[4]), "col")
+    totals = lax.psum(half, "row")
     factor = 1.0 / math.sqrt(CELLS)
     return (
         field.reshape(features.shape),

time: 862 us -> 831 us (0.964)
  waiting for transfers between devices: 196 us -> 161 us
    psum x1 -> x2, waiting for transfers between devices: 126 us -> 91.1 us  [the longest x1 56.7 us: per_device(): totals = lax.psum(half, 'row')]
    psum x1 -> x2, blocking collectives: 37.5 us -> 41.3 us  [the longest x1 26 us: per_device(): totals = lax.psum(half, 'row')]
  transfers between devices with their start and end apart: 3 -> 4, of which waited for: 3 -> 4; matrix products, arithmetic and copies ran while one was open for 0% -> 1% of each run, Pallas kernels for 0% -> 0%
where the time goes in v1:
time: 831 us; the launch traced here: 826 us
  matrix products  242 us (29%)
  local copies, waits for them, and re-layouts  208 us (25%)
  waiting for transfers between devices  161 us (19%)
  blocking collectives  143 us (17%)
  other arithmetic  46.9 us (6%)
  between operations  14.9 us (2%)
  starting transfers between devices  10 us (1%)
    dot_general x20, matrix products, contract(): jnp.einsum(form, left, right, precision=lax.Precision.HIGHEST, preferred_...  81.1 us
    unnamed x35, local copies, waits for them, and re-layouts  76.8 us
    all_to_all x1, blocking collectives, per_device(): lax.all_to_all(back_x, 'row', split_axis=4, concat_axis=5, tiled=True)  76 us
    psum x1, waiting for transfers between devices, per_device(): totals = lax.psum(half, 'row')  56.7 us
    all_to_all x1, waiting for transfers between devices, per_device(): lax.all_to_all(spectra, 'row', split_axis=4, concat_axis=5, tiled=True)  36.9 us
    dot_general x8, matrix products, closure_block(): jnp.einsum('fh,hn->fn', w_in, delta_in, preferred_element_type=jnp.float32)  34.8 us
    psum x1, waiting for transfers between devices, per_device(): half = lax.psum((local[0], local[1], local[2], local[3], local[4]), 'col')  34.3 us
    all_to_all x1, waiting for transfers between devices, per_device(): lax.all_to_all(stress_mid, 'col', split_axis=4, concat_axis=5, tiled=True)  33.1 us
  transfers between devices with their start and end apart: 4, of which 4 were waited for; matrix products, arithmetic and copies ran while one was open for 1% of the time, Pallas kernels for 0%

profile of v1, /device:TPU:0, one launch (start us, length us, event | category | flops | bytes accessed | tf_op | source)
XLA Modules:
  0.0 825.8 jit_solution(17693745026779628613)
XLA Ops:
  10.6 6.1 copy.51
  22.6 25.4 %all_to_all.60 = f32[4,1,98304]{2,1,0:T(1,128)S(1)} all-to-all(f32[4,1,98304]{2,1,0:T(1,128)} %reshape.562), channel_id=1, replica_groups=mesh['row'=8,'col'=4] {'col'}, dimensions={0} | all-to-all | bytes 3145728 | tf_op jit(solution)/shard_map/all_to_all | solution.py:82
  48.5 6.4 reduce.2
  54.8 6.2 reshape.563
  61.1 6.8 copy.95
  87.3 7.6 reshape.564
  100.8 36.9 %all-to-all-done.1 = f32[8,1,49152]{2,1,0:T(1,128)S(1)} async-done(((f32[8,1,49152]{2,1,0:T(1,128)}), f32[8,1,49152]{2,1,0:T(1,128)S(1)}, u32[]{:S(2)}, u32[]{:S(2)}) %all-to-all-start.1) | async-done | bytes 1572896 | tf_op jit(solution)/shard_map/all_to_all | solution.py:88
  137.7 6.2 reduce.3
  143.9 6.1 reshape.565
  186.6 11.4 %copy.63 = f32[2,6,1,32,128,16]{3,5,1,2,0,4:T(8,128)} copy(f32[2,6,1,32,128,16]{4,3,5,1,2,0:T(8,128)} %pad_maximum_fusion) | data formatting | bytes 6291456 | tf_op jit(solution)/shard_map/stack | solution.py:36
  198.1 10.7 %reshape.566 = f32[8,1,98304]{2,1,0:T(1,128)} reshape(f32[128,2,1,6,16,32]{5,4,3,2,1,0:T(8,128)} %bitcast.283) | data formatting | bytes 6291456
  208.7 76.0 %all_to_all.61 = f32[8,1,98304]{2,1,0:T(1,128)} all-to-all(f32[8,1,98304]{2,1,0:T(1,128)} %reshape.566), channel_id=1, replica_groups=mesh['row'=8,'col'=4] {'row'}, dimensions={0} | all-to-all | bytes 6291456 | tf_op jit(solution)/shard_map/all_to_all | solution.py:118
  284.7 11.7 %reduce.4 = f32[8,98304]{1,0:T(8,128)} reduce(f32[8,1,98304]{2,1,0:T(1,128)} %all_to_all.61, f32[]{:T(128)} %broadcast.808), dimensions={1}, to_apply=%all_to_all.50.reduce_sub_computation | reduce | bytes 6291460 | tf_op jit(solution)/shard_map/all_to_all | solution.py:118
  296.4 10.9 %reshape.567 = f32[128,2,1,6,16,32]{5,4,3,2,1,0:T(8,128)} reshape(f32[8,98304]{1,0:T(8,128)} %reduce.4) | data formatting | bytes 6291456
  307.3 10.4 %copy.64 = f32[2,6,1,32,128,16]{3,5,4,1,0,2:T(8,128)} copy(f32[2,6,1,32,128,16]{3,5,1,2,0,4:T(8,128)} %bitcast.281) | data formatting | bytes 6291456 | tf_op jit(solution)/shard_map/all_to_all | solution.py:118
  317.6 10.7 %fusion.205 = (f32[1,6,1,32,16,8,16]{3,6,4,5,1,0,2:T(8,128)}, f32[1,6,1,32,16,8,16]{3,6,4,5,1,0,2:T(8,128)}) fusion(f32[2,6,1,32,16,8,16]{3,6,4,5,1,0,2:T(8,128)} %bitcast.279), kind=kLoop, calls=%fused_computation.273 | loop fusion | bytes 6291456 | tf_op jit(solution)/shard_map/slice | solution.py:34
  332.1 10.1 %fusion.64 = f32[128,6,32,16]{0,2,3,1:T(8,128)S(1)} fusion(f32[6,32,16,128]{1,3,2,0:T(8,128)S(1)} %bitcast.277, s32[128]{0:T(128)S(1)} %compare_select_fusion), kind=kOutput, calls=%fused_computation.138 | convolution fusion | flops 604225536 | bytes 3146240 | tf_op jit(solution)/shard_map/cskxq,qy->csxyk/dot_general | solution.py:28
  342.2 10.2 %fusion.43 = f32[128,6,32,16]{0,2,3,1:T(8,128)S(1)} fusion(f32[6,32,16,128]{1,3,2,0:T(8,128)S(1)} %bitcast.278, s32[128]{0:T(128)S(1)} %compare_select_fusion), kind=kOutput, calls=%fused_computation.117 | convolution fusion | flops 604225536 | bytes 3146240 | tf_op jit(solution)/shard_map/cskxq,qy->csxyk/dot_general | solution.py:28
  353.4 10.5 %subtract_bitcast_fusion = f32[1,6,1,16,128,32]{4,5,3,1,2,0:T(8,128)S(1)} fusion(f32[128,6,32,16]{0,2,3,1:T(8,128)S(1)} %fusion.64, f32[6,32,16,128]{1,3,2,0:T(8,128)S(1)} %bitcast.275, s32[128]{0:T(128)S(1)} %compare_select_fusion), kind=kOutput, calls=%fused_computation.41 | convolution fusion | flops 604618752 | bytes 4719104 | tf_op jit(solution)/shard_map/cskxq,qy->csxyk/dot_general | solution.py:28
  363.9 10.1 %add_bitcast_fusion = f32[1,6,1,16,128,32]{4,5,3,1,2,0:T(8,128)S(1)} fusion(f32[128,6,32,16]{0,2,3,1:T(8,128)S(1)} %fusion.43, f32[6,32,16,128]{1,3,2,0:T(8,128)S(1)} %bitcast.276, s32[128]{0:T(128)S(1)} %compare_select_fusion), kind=kOutput, calls=%fused_computation.40 | convolution fusion | flops 604618752 | bytes 4719104 | tf_op jit(solution)/shard_map/cskxq,qy->csxyk/dot_general | solution.py:28
  376.0 11.4 %copy.71 = f32[2,6,1,16,128,32]{5,3,1,2,0,4:T(8,128)} copy(f32[2,6,1,16,128,32]{4,5,3,1,2,0:T(8,128)} %pad_maximum_fusion.1) | data formatting | bytes 6291456 | tf_op jit(solution)/shard_map/stack | solution.py:36
  387.4 9.3 %reshape.568 = f32[4,1,196608]{2,1,0:T(1,128)} reshape(f32[128,2,1,6,16,32]{5,4,3,2,1,0:T(8,128)} %bitcast.284) | data formatting | bytes 6291456
  404.5 33.1 %all-to-all-done.3 = f32[4,1,196608]{2,1,0:T(1,128)} async-done(((f32[4,1,196608]{2,1,0:T(1,128)}), f32[4,1,196608]{2,1,0:T(1,128)}, u32[]{:S(2)}, u32[]{:S(2)}) %all-to-all-start.3) | async-done | bytes 3145760 | tf_op jit(solution)/shard_map/all_to_all | solution.py:124
  437.6 11.8 %reduce.5 = f32[4,196608]{1,0:T(4,128)} reduce(f32[4,1,196608]{2,1,0:T(1,128)} %all-to-all-done.3, f32[]{:T(128)} %broadcast.808), dimensions={1}, to_apply=%all_to_all.53.reduce_sub_computation | reduce | bytes 6291460 | tf_op jit(solution)/shard_map/all_to_all | solution.py:124
  449.4 10.7 %reshape.569 = f32[128,2,1,6,16,32]{5,4,3,2,1,0:T(8,128)} reshape(f32[4,196608]{1,0:T(4,128)} %reduce.5) | data formatting | bytes 6291456
  460.2 16.4 %copy.94 = f32[2,6,1,16,4,32,32]{6,4,5,3,1,2,0:T(4,128)} copy(f32[2,6,1,16,4,32,32]{6,3,1,0,5,4,2:T(8,128)} %bitcast.282) | data formatting | bytes 6291456 | tf_op jit(solution)/shard_map/all_to_all | solution.py:124
  476.6 14.3 %fusion.204 = (f32[1,6,1,16,32,4,32]{6,5,4,3,1,2,0:T(4,128)}, f32[1,6,1,16,32,4,32]{6,5,4,3,1,2,0:T(4,128)}) fusion(f32[2,6,1,16,32,4,32]{6,5,4,3,1,2,0:T(4,128)} %bitcast.280), kind=kLoop, calls=%fused_computation.272 | loop fusion | bytes 6291456 | tf_op jit(solution)/shard_map/slice | solution.py:126
  511.8 165.7 %while.24 = (s32[]{:T(128)}, f32[9,65536]{1,0:T(8,128)}, f32[9,256]{1,0:T(8,128)S(1)}, f32[256]{0:T(256)S(1)}, f32[256,256]{1,0:T(8,128)S(1)}, /*index=5*/f32[25...) while((s32[]{:T(128)}, f32[9,65536]{1,0:T(8,128)}, ...), condition=%wide.region_3.4_spmd.clone, body=%wide.region_0.3_spmd.clone.sunk | while | flops 3422691328 | bytes 157343136 | solution.py:153
  677.4 15.3 %all-reduce.1 = (f32[9,256]{1,0:T(8,128)S(1)}, f32[256]{0:T(256)S(1)}, f32[256]{0:T(256)S(1)}, f32[256,6]{0,1:T(8,128)S(1)}) all-reduce(f32[9,256]{1,0:T(8,128)S(1)} %get-tuple-element.241, f32[256]{0:T(256)S(1)} %get-tuple-element.242, f32[256]{0:T(256)S(1)} %get-tuple-element.244, ...), channel_id=1, replica_groups=mesh['row'=8,'col'=4] {'col'}, use_global_device_ids=true, to_apply=%region_4.5 | all-reduce | flops 4352 | bytes 34816 | tf_op jit(solution)/shard_map/psum | solution.py:154
  692.8 26.0 %all-reduce = (f32[9,256]{1,0:T(8,128)S(1)}, f32[256]{0:T(256)S(1)}, f32[256]{0:T(256)S(1)}, f32[256,6]{0,1:T(8,128)S(1)}) all-reduce(f32[9,256]{1,0:T(8,128)S(1)} %get-tuple-element.323, f32[256]{0:T(256)S(1)} %get-tuple-element.324, f32[256]{0:T(256)S(1)} %get-tuple-element.325, ...), channel_id=1, replica_groups=mesh['row'=8,'col'=4] {'row'}, use_global_device_ids=true, to_apply=%region_5.6 | all-reduce | flops 4352 | bytes 34816 | tf_op jit(solution)/shard_map/psum | solution.py:155
  725.3 34.3 %all-reduce.5.cloned.1.call-done = f32[256,256]{1,0:T(8,128)} async-done(((f32[256,256]{1,0:T(8,128)}), f32[256,256]{1,0:T(8,128)}) %all-reduce.5.cloned.1.call-update) | async-done | bytes 262160 | tf_op jit(solution)/shard_map/psum | solution.py:154
  760.2 56.7 %all-reduce.7.cloned.1.call-done = f32[256,256]{1,0:T(8,128)} async-done(((f32[256,256]{1,0:T(8,128)}), f32[256,256]{1,0:T(8,128)}) %all-reduce.7.cloned.1.call-update) | async-done | bytes 262160 | tf_op jit(solution)/shard_map/psum | solution.py:155
  (272 shorter events, 280.0 us)
Async XLA Ops:
  94.9 42.8 %all-to-all-start.1 = ((f32[8,1,49152]{2,1,0:T(1,128)}), f32[8,1,49152]{2,1,0:T(1,128)S(1)}, u32[]{:S(2)}, u32[]{:S(2)}) async-start(f32[8,1,49152]{2,1,0:T(1,128)} %reshape.564), calls=%async_computation.1 | async-start | bytes 3145728 | tf_op jit(solution)/shard_map/all_to_all | solution.py:88
  332.1 20.3 %slice-start = ((s8[6291456]{0:T(1024)(128)(4,1)}), s8[4194304]{0:T(1024)(128)(4,1)S(1)}, s32[]{:S(2)}) async-start(s8[6291456]{0:T(1024)(128)(4,1)} %bitcast.291), calls=%async_computation.6 | async-start | bytes 8388608
  342.1 10.3 %slice-start.1 = ((s8[6291456]{0:T(1024)(128)(4,1)}), s8[2097152]{0:T(1024)(128)(4,1)S(1)}, s32[]{:S(2)}) async-start(s8[6291456]{0:T(1024)(128)(4,1)} %bitcast.291), calls=%async_computation.7 | async-start | bytes 4194304
  396.7 4.9 copy-start.9
  396.7 40.9 %all-to-all-start.3 = ((f32[4,1,196608]{2,1,0:T(1,128)}), f32[4,1,196608]{2,1,0:T(1,128)}, u32[]{:S(2)}, u32[]{:S(2)}) async-start(f32[4,1,196608]{2,1,0:T(1,128)} %reshape.568), calls=%async_computation.3 | async-start | bytes 6291456 | tf_op jit(solution)/shard_map/all_to_all | solution.py:124
  401.5 358.1 %all-reduce.5.cloned.1.call-start = ((), (), s32[]{:S(2)}) async-start(), calls=%async_computation.4 | async-start | bytes 524288 | tf_op jit(solution)/shard_map/psum | solution.py:154
  517.8 4.0 copy-start.5
  521.7 4.4 copy-start.4
  538.4 4.0 copy-start.5
  542.4 4.4 copy-start.4
  546.8 3.7 copy-start.2
  559.1 4.0 copy-start.5
  563.1 4.4 copy-start.4
  567.4 3.7 copy-start.2
  579.8 4.0 copy-start.5
  583.7 4.3 copy-start.4
  588.1 3.7 copy-start.2
  600.4 4.0 copy-start.5
  604.4 4.4 copy-start.4
  608.8 3.7 copy-start.2
  621.1 4.0 copy-start.5
  625.1 4.4 copy-start.4
  629.5 3.7 copy-start.2
  641.8 4.0 copy-start.5
  645.8 4.4 copy-start.4
  650.1 3.7 copy-start.2
  662.5 4.0 copy-start.5
  666.4 4.3 copy-start.4
  670.8 3.7 copy-start.2
  677.4 41.9 %copy-start.8 = (f32[256,256]{1,0:T(8,128)}, f32[256,256]{1,0:T(8,128)S(1)}, u32[]{:S(2)}) copy-start(f32[256,256]{1,0:T(8,128)S(1)} %get-tuple-element.243) | copy-start | bytes 786436
  719.4 97.6 %all-reduce.7.cloned.1.call-start = ((), (), s32[]{:S(2)}) async-start(), calls=%async_computation.5 | async-start | bytes 524288 | tf_op jit(solution)/shard_map/psum | solution.py:155
  720.0 98.7 %copy-start.1 = (f32[3,1,16,32,128]{4,3,2,1,0:T(8,128)S(1)}, f32[3,1,16,32,128]{4,3,2,1,0:T(8,128)}, u32[]{:S(2)}) copy-start(f32[3,1,16,32,128]{4,3,2,1,0:T(8,128)} %param.10) | copy-start | bytes 2359300
  (31 other events, 80.4 us)
Sparse Core Ops, SparseCore 0:
  719.5 40.1 all-reduce.4
  762.1 54.8 all-reduce.6
